TPU v7x, 256 devices: a whole 4x4x8 slice. The times are simulated.
256 devices in a mesh: freq: 64 (over y, z, x_hi), inp: 4 (over x_lo, core).
Axes of the slice: x: 4 (x_hi: 2, x_lo: 2; x = x_hi * 2 + x_lo), y: 4, z: 8, core: 2. Of those that a mesh axis runs over, the one named last changes fastest.
Arguments:
- voltages: int32 [192, 2048, 1024], P('freq', None, 'inp'), may hold values from -128 to 127
- taps: float32 [12, 2048], replicated, may hold values from -0.013671875 to 0.013671875
- start: int32 [8, 2, 1024], replicated, may hold values from -127 to 127
Outputs:
- cleaned: bfloat16 [1024, 192, 2, 1024], P('freq', None, None, 'inp')
- ritz_matrix: float32 [1024, 8, 8], P('freq')
Inputs may be any that keep to these rules, and one draw needn't show every extreme that they name: `voltages`: 8-bit voltage samples.
All inputs are finite; a program needn't handle non-finite values.
Results may differ from a plain program's by a relative error of at most 0.0052.
Values may be sent and summed in bfloat16 or wider, within the bound.
No kernel may reach another device: no remote copies, remote signals or barrier semaphores. Data moves between devices by JAX's collectives and lax.ppermute only.
A program may use at most 192 MiB of HBM per device.

v0:
```python
import math
import jax
import jax.numpy as jnp
from jax import lax
from jax.sharding import PartitionSpec as P

ITERS = 4


def from_behind(value, axis, steps):
    count = lax.axis_size(axis)
    pairs = [(source, (source + steps) % count) for source in range(count)]
    return lax.ppermute(value, axis, pairs)


def project_rows(basis_rows, channel_data):
    projected = jnp.einsum(
        "ckr,cmr->ckm", basis_rows, channel_data, precision=lax.Precision.HIGHEST
    )
    return lax.psum(projected, "inp")


def subspace_clean(turned, start_block):
    highest = lax.Precision.HIGHEST
    channel_local, spectra_count, part_count, inputs_width = turned.shape
    row_count = part_count * inputs_width
    channel_data = turned.reshape(channel_local, spectra_count, row_count).astype(jnp.float32)
    start_rows = start_block.reshape(start_block.shape[0], row_count).astype(jnp.float32)
    basis_rows = jnp.broadcast_to(start_rows[None], (channel_local,) + start_rows.shape)
    for iteration in range(ITERS):
        projected = project_rows(basis_rows, channel_data)
        mapped = (
            jnp.einsum("ckm,cmr->ckr", projected, channel_data, precision=highest) / spectra_count
        )
        gram_matrix = jnp.einsum("ckr,cjr->ckj", mapped, mapped, precision=highest)
        gram_matrix = lax.psum(gram_matrix, "inp")
        lower_factor = jnp.linalg.cholesky(gram_matrix)
        basis_rows = lax.linalg.triangular_solve(lower_factor, mapped, left_side=True, lower=True)
    projected = project_rows(basis_rows, channel_data)
    ritz_matrix = (
        jnp.einsum("ckm,cjm->ckj", projected, projected, precision=highest) / spectra_count
    )
    cleaned = channel_data - jnp.einsum("ckm,ckr->cmr", projected, basis_rows, precision=highest)
    cleaned = cleaned.reshape(channel_local, spectra_count, part_count, inputs_width).astype(
        jnp.bfloat16
    )
    return (cleaned, ritz_matrix)


def shards(voltages, taps, start):
    slot_count = voltages.shape[0]
    frame_len = voltages.shape[1]
    inputs_local = voltages.shape[2]
    channel_count = frame_len // 2
    tap_count = taps.shape[0]
    frame_stack = voltages.astype(jnp.bfloat16)
    history_len = tap_count - 1
    group_count = lax.axis_size("freq")
    portions = [frame_stack]
    shift_count = (history_len - 1) // slot_count + 1
    for distance in range(1, shift_count + 1):
        first_frame = max(0, distance * slot_count - history_len)
        portion = frame_stack[first_frame:]
        offset_mod = distance % group_count
        arrived = from_behind(portion, "freq", offset_mod)
        portions = [arrived] + portions
    extended = jnp.concatenate(portions, axis=0)
    filtered = jnp.zeros((slot_count, frame_len, inputs_local), jnp.float32)
    for tap_index in range(tap_count):
        window = extended[tap_index : tap_index + slot_count].astype(jnp.float32)
        filtered = filtered + taps[tap_index][None, :, None] * window
    channel_idx = lax.broadcasted_iota(jnp.int32, (channel_count, frame_len), 0)
    sample_idx = lax.broadcasted_iota(jnp.int32, (channel_count, frame_len), 1)
    angles = (channel_idx * sample_idx % frame_len).astype(jnp.float32) * (
        2.0 * math.pi / frame_len
    )
    dft_scale = 1.0 / math.sqrt(channel_count)
    cosine = jnp.cos(angles)
    sine_table = jnp.sin(angles)
    real_part = (
        jnp.einsum("kn,sni->ksi", cosine, filtered, precision=lax.Precision.HIGHEST) * dft_scale
    )
    imag_part = (
        -jnp.einsum("kn,sni->ksi", sine_table, filtered, precision=lax.Precision.HIGHEST)
        * dft_scale
    )
    spectra = jnp.stack([real_part, imag_part], axis=2).astype(jnp.bfloat16)
    turned = lax.all_to_all(spectra, "freq", split_axis=0, concat_axis=1, tiled=True)
    start_local = lax.dynamic_slice_in_dim(
        start, lax.axis_index("inp") * inputs_local, inputs_local, 2
    )
    cleaned, ritz_matrix = subspace_clean(turned, start_local)
    return (cleaned, ritz_matrix)


def solution(mesh):
    placed = (P("freq", None, "inp"), P(), P())
    return jax.shard_map(
        shards,
        mesh=mesh,
        in_specs=placed,
        out_specs=(P("freq", None, None, "inp"), P("freq", None, None)),
        check_vma=False,
    )
```

profile of v0, /device:TPU:1, one launch (start us, length us, event | category | flops | bytes accessed | tf_op | source)
XLA Modules:
  0.0 1002.1 jit_solution(7785082553652282310)
XLA Ops:
  22.3 181.6 %collective-permute-done = bf16[2,2048,256]{2,1,0:T(8,128)(2,1)S(1)} collective-permute-done((bf16[2,2048,256]{2,1,0:T(8,128)(2,1)S(1)}, bf16[2,2048,256]{2,1,0:T(8,128)(2,1)S(1)}, u32[]{:S(2)}, u32[]{:S(2)}) %collective-permute-start) | collective-permute-done | bytes 2097184 | tf_op jit(solution)/shard_map/ppermute | solution.py:13
  204.6 16.6 %collective-permute-done.2 = bf16[3,2048,256]{2,1,0:T(8,128)(2,1)S(1)} collective-permute-done((bf16[3,2048,256]{2,1,0:T(8,128)(2,1)S(1)}, bf16[3,2048,256]{2,1,0:T(8,128)(2,1)S(1)}, u32[]{:S(2)}, u32[]{:S(2)}) %collective-permute-start.2) | collective-permute-done | bytes 3145760 | tf_op jit(solution)/shard_map/ppermute | solution.py:13
  221.6 70.7 %collective-permute-done.3 = bf16[3,2048,256]{2,1,0:T(8,128)(2,1)S(1)} collective-permute-done((bf16[3,2048,256]{2,1,0:T(8,128)(2,1)S(1)}, bf16[3,2048,256]{2,1,0:T(8,128)(2,1)S(1)}, u32[]{:S(2)}, u32[]{:S(2)}) %collective-permute-start.3) | collective-permute-done | bytes 3145760 | tf_op jit(solution)/shard_map/ppermute | solution.py:13
  302.2 64.8 %fusion.19 = bf16[1024,3,1,256]{3,0,1,2:T(8,128)(2,1)S(1)} fusion(f32[3,2048,256]{2,1,0:T(8,128)} %multiply_add_fusion), kind=kOutput, calls=%fused_computation.25 | convolution fusion | flops 19358285824 | bytes 7864320 | tf_op jit(solution)/shard_map/kn,sni->ksi/dot_general | solution.py:81
  367.0 53.0 %fusion.22 = bf16[1024,3,1,256]{3,0,1,2:T(8,128)(2,1)S(1)} fusion(f32[3,2048,256]{2,1,0:T(8,128)S(1)} %copy-done), kind=kOutput, calls=%fused_computation.26 | convolution fusion | flops 19359072256 | bytes 7864320 | tf_op jit(solution)/shard_map/kn,sni->ksi/dot_general | solution.py:84
  425.2 98.1 %all-to-all-start = ((bf16[1024,3,2,256]{3,2,1,0:T(2,128)(2,1)}), bf16[1024,3,2,256]{3,2,1,0:T(2,128)(2,1)S(1)}, u32[]{:S(2)}, u32[]{:S(2)}) async-start(bf16[1024,3,2,256]{3,2,1,0:T(2,128)(2,1)} %copy.77), calls=%async_computation | async-start | bytes 6291456 | tf_op jit(solution)/shard_map/all_to_all | solution.py:88
  524.1 71.6 %all-to-all-done = bf16[1024,3,2,256]{3,2,1,0:T(2,128)(2,1)S(1)} async-done(((bf16[1024,3,2,256]{3,2,1,0:T(2,128)(2,1)}), bf16[1024,3,2,256]{3,2,1,0:T(2,128)(2,1)S(1)}, u32[]{:S(2)}, u32[]{:S(2)}) %all-to-all-start) | async-done | bytes 3145760 | tf_op jit(solution)/shard_map/all_to_all | solution.py:88
  608.3 38.9 %all-reduce.6.cloned.1.call-done = f32[16,8,192]{2,1,0:T(8,128)} async-done(((f32[16,8,192]{2,1,0:T(8,128)}), f32[16,8,192]{2,1,0:T(8,128)}) %all-reduce.6.cloned.1.call-update) | async-done | bytes 98320 | tf_op jit(solution)/shard_map/psum | solution.py:20
  650.1 10.6 %psum.64 = f32[16,8,8]{1,2,0:T(8,128)S(1)} all-reduce(f32[16,8,8]{1,2,0:T(8,128)S(1)} %fusion.48), channel_id=1, replica_groups=mesh['freq'=64,'inp'=4] {'inp'}, use_global_device_ids=true, to_apply=%region_1.2 | all-reduce | flops 1024 | bytes 8192 | tf_op jit(solution)/shard_map/psum | solution.py:36
  661.4 12.4 %custom-call.12 = f32[16,8,8]{2,1,0:T(8,128)S(1)} custom-call(f32[16,8,8]{2,1,0:T(8,128)} %fusion.38), custom_call_target="Cholesky" | custom-call | tf_op jit(solution)/shard_map/jit(cholesky)/cholesky | solution.py:37
  674.1 10.0 custom-call.13
  688.3 42.2 %all-reduce.8.cloned.1.call-done = f32[16,8,192]{2,1,0:T(8,128)} async-done(((f32[16,8,192]{2,1,0:T(8,128)}), f32[16,8,192]{2,1,0:T(8,128)}) %all-reduce.8.cloned.1.call-update) | async-done | bytes 98320 | tf_op jit(solution)/shard_map/psum | solution.py:20
  733.3 10.6 %psum.66 = f32[16,8,8]{1,2,0:T(8,128)S(1)} all-reduce(f32[16,8,8]{1,2,0:T(8,128)S(1)} %fusion.50), channel_id=1, replica_groups=mesh['freq'=64,'inp'=4] {'inp'}, use_global_device_ids=true, to_apply=%region_5.8 | all-reduce | flops 1024 | bytes 8192 | tf_op jit(solution)/shard_map/psum | solution.py:36
  744.7 12.4 %custom-call.14 = f32[16,8,8]{2,1,0:T(8,128)S(1)} custom-call(f32[16,8,8]{2,1,0:T(8,128)} %fusion.35), custom_call_target="Cholesky" | custom-call | tf_op jit(solution)/shard_map/jit(cholesky)/cholesky | solution.py:37
  757.3 10.0 custom-call.15
  771.1 42.6 %all-reduce.10.cloned.1.call-done = f32[16,8,192]{2,1,0:T(8,128)} async-done(((f32[16,8,192]{2,1,0:T(8,128)}), f32[16,8,192]{2,1,0:T(8,128)}) %all-reduce.10.cloned.1.call-update) | async-done | bytes 98320 | tf_op jit(solution)/shard_map/psum | solution.py:20
  816.6 10.6 %psum.68 = f32[16,8,8]{1,2,0:T(8,128)S(1)} all-reduce(f32[16,8,8]{1,2,0:T(8,128)S(1)} %fusion.52), channel_id=1, replica_groups=mesh['freq'=64,'inp'=4] {'inp'}, use_global_device_ids=true, to_apply=%region_7.10 | all-reduce | flops 1024 | bytes 8192 | tf_op jit(solution)/shard_map/psum | solution.py:36
  827.9 12.4 %custom-call.16 = f32[16,8,8]{2,1,0:T(8,128)S(1)} custom-call(f32[16,8,8]{2,1,0:T(8,128)} %fusion.32), custom_call_target="Cholesky" | custom-call | tf_op jit(solution)/shard_map/jit(cholesky)/cholesky | solution.py:37
  840.6 10.0 custom-call.17
  854.4 42.6 %all-reduce.12.cloned.1.call-done = f32[16,8,192]{2,1,0:T(8,128)} async-done(((f32[16,8,192]{2,1,0:T(8,128)}), f32[16,8,192]{2,1,0:T(8,128)}) %all-reduce.12.cloned.1.call-update) | async-done | bytes 98320 | tf_op jit(solution)/shard_map/psum | solution.py:20
  899.9 10.8 %psum.70 = f32[16,8,8]{1,2,0:T(8,128)S(1)} all-reduce(f32[16,8,8]{1,2,0:T(8,128)S(1)} %fusion.54), channel_id=1, replica_groups=mesh['freq'=64,'inp'=4] {'inp'}, use_global_device_ids=true, to_apply=%region_9.12 | all-reduce | flops 1024 | bytes 8192 | tf_op jit(solution)/shard_map/psum | solution.py:36
  911.4 12.4 %custom-call.18 = f32[16,8,8]{2,1,0:T(8,128)S(1)} custom-call(f32[16,8,8]{2,1,0:T(8,128)} %fusion.29), custom_call_target="Cholesky" | custom-call | tf_op jit(solution)/shard_map/jit(cholesky)/cholesky | solution.py:37
  924.0 10.0 custom-call.19
  938.5 42.7 %all-reduce.14.cloned.1.call-done = f32[16,8,192]{2,1,0:T(8,128)} async-done(((f32[16,8,192]{2,1,0:T(8,128)}), f32[16,8,192]{2,1,0:T(8,128)}) %all-reduce.14.cloned.1.call-update) | async-done | bytes 98320 | tf_op jit(solution)/shard_map/psum | solution.py:20
  (84 shorter events, 90.0 us)
Async XLA Ops:
  7.2 15.1 %copy-start.3 = (f32[12,2048]{1,0:T(8,128)S(1)}, f32[12,2048]{1,0:T(8,128)}, u32[]{:S(2)}) copy-start(f32[12,2048]{1,0:T(8,128)} %param.7) | copy-start | bytes 294916
  10.5 193.6 %collective-permute-start.1 = (bf16[3,2048,256]{2,1,0:T(8,128)(2,1)S(1)}, bf16[3,2048,256]{2,1,0:T(8,128)(2,1)S(1)}, u32[]{:S(2)}, u32[]{:S(2)}) collective-permute-start(bf16[3,2048,256]{2,1,0:T(8,128)(2,1)S(1)} %convert_element_type.65), channel_id=1, source_target_pairs={{0,12},{4,16},{8,20},{12,24},{16,28},{20,32},{24,36},{28,40},{32,4... | collective-permute-start | bytes 9437192 | tf_op jit(solution)/shard_map/ppermute | solution.py:13
  15.5 205.7 %collective-permute-start.2 = (bf16[3,2048,256]{2,1,0:T(8,128)(2,1)S(1)}, bf16[3,2048,256]{2,1,0:T(8,128)(2,1)S(1)}, u32[]{:S(2)}, u32[]{:S(2)}) collective-permute-start(bf16[3,2048,256]{2,1,0:T(8,128)(2,1)S(1)} %convert_element_type.65), channel_id=1, source_target_pairs={{0,8},{4,12},{8,16},{12,20},{16,24},{20,28},{24,32},{28,36},{32,40... | collective-permute-start | bytes 9437192 | tf_op jit(solution)/shard_map/ppermute | solution.py:13
  17.2 275.1 %collective-permute-start.3 = (bf16[3,2048,256]{2,1,0:T(8,128)(2,1)S(1)}, bf16[3,2048,256]{2,1,0:T(8,128)(2,1)S(1)}, u32[]{:S(2)}, u32[]{:S(2)}) collective-permute-start(bf16[3,2048,256]{2,1,0:T(8,128)(2,1)S(1)} %convert_element_type.65), channel_id=1, source_target_pairs={{0,4},{4,8},{8,12},{12,16},{16,20},{20,24},{24,28},{28,32},{32,36}... | collective-permute-start | bytes 9437192 | tf_op jit(solution)/shard_map/ppermute | solution.py:13
  18.9 185.1 %collective-permute-start = (bf16[2,2048,256]{2,1,0:T(8,128)(2,1)S(1)}, bf16[2,2048,256]{2,1,0:T(8,128)(2,1)S(1)}, u32[]{:S(2)}, u32[]{:S(2)}) collective-permute-start(bf16[2,2048,256]{2,1,0:T(8,128)(2,1)S(1)} %slice.98), channel_id=1, source_target_pairs={{0,16},{4,20},{8,24},{12,28},{16,32},{20,36},{24,40},{28,44},{32,4... | collective-permute-start | bytes 6291464 | tf_op jit(solution)/shard_map/ppermute | solution.py:13
  302.2 64.8 %copy-start = (f32[3,2048,256]{2,1,0:T(8,128)S(1)}, f32[3,2048,256]{2,1,0:T(8,128)}, u32[]{:S(2)}) copy-start(f32[3,2048,256]{2,1,0:T(8,128)} %multiply_add_fusion) | copy-start | bytes 18874372
  425.2 170.6 %all-to-all-start = ((bf16[1024,3,2,256]{3,2,1,0:T(2,128)(2,1)}), bf16[1024,3,2,256]{3,2,1,0:T(2,128)(2,1)S(1)}, u32[]{:S(2)}, u32[]{:S(2)}) async-start(bf16[1024,3,2,256]{3,2,1,0:T(2,128)(2,1)} %copy.77), calls=%async_computation | async-start | bytes 6291456 | tf_op jit(solution)/shard_map/all_to_all | solution.py:88
  523.3 123.9 %all-reduce.6.cloned.1.call-start = ((), (), s32[]{:S(2)}) async-start(), calls=%async_computation.1 | async-start | bytes 262144 | tf_op jit(solution)/shard_map/psum | solution.py:20
  608.2 122.3 %all-reduce.8.cloned.1.call-start = ((), (), s32[]{:S(2)}) async-start(), calls=%async_computation.2 | async-start | bytes 262144 | tf_op jit(solution)/shard_map/psum | solution.py:20
  687.8 126.0 %all-reduce.10.cloned.1.call-start = ((), (), s32[]{:S(2)}) async-start(), calls=%async_computation.3 | async-start | bytes 262144 | tf_op jit(solution)/shard_map/psum | solution.py:20
  771.1 126.0 %all-reduce.12.cloned.1.call-start = ((), (), s32[]{:S(2)}) async-start(), calls=%async_computation.4 | async-start | bytes 262144 | tf_op jit(solution)/shard_map/psum | solution.py:20
  854.3 126.8 %all-reduce.14.cloned.1.call-start = ((), (), s32[]{:S(2)}) async-start(), calls=%async_computation.5 | async-start | bytes 262144 | tf_op jit(solution)/shard_map/psum | solution.py:20
  934.6 0.7 copy-start.1
  981.2 13.2 %copy-start.2 = (f32[16,8,192]{2,1,0:T(8,128)S(1)}, f32[16,8,192]{2,1,0:T(8,128)}, u32[]{:S(2)}) copy-start(f32[16,8,192]{2,1,0:T(8,128)} %all-reduce.14.cloned.1.call-done) | copy-start | bytes 294916
Sparse Core Ops, SparseCore 0:
  608.4 38.8 all-reduce.5
  687.9 42.5 all-reduce.7
  771.2 42.5 all-reduce.9
  854.4 42.5 all-reduce.11
  938.6 42.5 all-reduce.13
where the time goes:
time: 1010 us; the launch traced here: 1000 us
  waiting for transfers between devices  550 us (54%)
  matrix products  155 us (15%)
  starting transfers between devices  110 us (11%)
  other arithmetic  107 us (11%)
  blocking collectives  42.7 us (4%)
  local copies, waits for them, and re-layouts  23 us (2%)
  between operations  14.2 us (1%)
    ppermute x4, waiting for transfers between devices, from_behind(): return lax.ppermute(value, axis, pairs)  269 us
    psum x5, waiting for transfers between devices, project_rows(): return lax.psum(projected, 'inp')  209 us
    all_to_all x1, starting transfers between devices, shards(): lax.all_to_all(spectra, 'freq', split_axis=0, concat_axis=1, tiled=True)  98.1 us
    all_to_all x1, waiting for transfers between devices, shards(): lax.all_to_all(spectra, 'freq', split_axis=0, concat_axis=1, tiled=True)  71.6 us
    dot_general x1, matrix products, shards(): jnp.einsum('kn,sni->ksi', cosine, filtered, precision=lax.Precision.HIGHEST)  64.8 us
    dot_general x1, matrix products, shards(): jnp.einsum('kn,sni->ksi', sine_table, filtered, precision=lax.Precision.H...  53 us
    another operation x13, other arithmetic, subspace_clean(): lower_factor = jnp.linalg.cholesky(gram_matrix)  49.9 us
    psum x4, blocking collectives, subspace_clean(): gram_matrix = lax.psum(gram_matrix, 'inp')  42.7 us
  transfers between devices with their start and end apart: 10, of which 9 were waited for; matrix products, arithmetic and copies ran while one was open for 0% of the time, Pallas kernels for 0%

commit v1 on v0

--- a/solution.py
+++ b/solution.py
@@ -17,7 +17,7 @@
     projected = jnp.einsum(
         "ckr,cmr->ckm", basis_rows, channel_data, precision=lax.Precision.HIGHEST
     )
-    return lax.psum(projected, "inp")
+    return jnp.sum(lax.all_gather(projected, "inp"), axis=0)
 
 
 def subspace_clean(turned, start_block):

time: 1010 us -> 828 us (0.82)
  waiting for transfers between devices: 550 us -> 341 us
  blocking collectives: 42.7 us -> 86.3 us
  between operations: 14.2 us -> 1.12 us
    psum x5 -> x0, waiting for transfers between devices: 209 us -> none  [project_rows(): return lax.psum(projected, 'inp')]
    all_gather x0 -> x5, blocking collectives: none -> 43.9 us  [project_rows(): return jnp.sum(lax.all_gather(projected, 'inp'), axis=0)]
  transfers between devices with their start and end apart: 10 -> 5, of which waited for: 9 -> 4; matrix products, arithmetic and copies ran while one was open for 0% -> 0% of each run, Pallas kernels for 0% -> 0%
where the time goes in v1:
time: 828 us; the launch traced here: 821 us
  waiting for transfers between devices  341 us (41%)
  matrix products  148 us (18%)
  other arithmetic  112 us (14%)
  starting transfers between devices  110 us (13%)
  blocking collectives  86.3 us (10%)
  local copies, waits for them, and re-layouts  23 us (3%)
    ppermute x4, waiting for transfers between devices, from_behind(): return lax.ppermute(value, axis, pairs)  269 us
    all_to_all x1, starting transfers between devices, shards(): lax.all_to_all(spectra, 'freq', split_axis=0, concat_axis=1, tiled=True)  98.1 us
    all_to_all x1, waiting for transfers between devices, shards(): lax.all_to_all(spectra, 'freq', split_axis=0, concat_axis=1, tiled=True)  71.7 us
    dot_general x1, matrix products, shards(): jnp.einsum('kn,sni->ksi', cosine, filtered, precision=lax.Precision.HIGHEST)  64.8 us
    dot_general x1, matrix products, shards(): jnp.einsum('kn,sni->ksi', sine_table, filtered, precision=lax.Precision.H...  53 us
    another operation x13, other arithmetic, subspace_clean(): lower_factor = jnp.linalg.cholesky(gram_matrix)  49.9 us
    all_gather x5, blocking collectives, project_rows(): return jnp.sum(lax.all_gather(projected, 'inp'), axis=0)  43.9 us
    psum x4, blocking collectives, subspace_clean(): gram_matrix = lax.psum(gram_matrix, 'inp')  42.5 us
  transfers between devices with their start and end apart: 5, of which 4 were waited for; matrix products, arithmetic and copies ran while one was open for 0% of the time, Pallas kernels for 0%

profile of v1, /device:TPU:1, one launch (start us, length us, event | category | flops | bytes accessed | tf_op | source)
XLA Modules:
  0.0 821.1 jit_solution(7553258419217040100)
XLA Ops:
  15.8 181.6 %collective-permute-done = bf16[2,2048,256]{2,1,0:T(8,128)(2,1)S(1)} collective-permute-done((bf16[2,2048,256]{2,1,0:T(8,128)(2,1)S(1)}, bf16[2,2048,256]{2,1,0:T(8,128)(2,1)S(1)}, u32[]{:S(2)}, u32[]{:S(2)}) %collective-permute-start) | collective-permute-done | bytes 2097184 | tf_op jit(solution)/shard_map/ppermute | solution.py:13
  198.0 16.6 %collective-permute-done.2 = bf16[3,2048,256]{2,1,0:T(8,128)(2,1)S(1)} collective-permute-done((bf16[3,2048,256]{2,1,0:T(8,128)(2,1)S(1)}, bf16[3,2048,256]{2,1,0:T(8,128)(2,1)S(1)}, u32[]{:S(2)}, u32[]{:S(2)}) %collective-permute-start.2) | collective-permute-done | bytes 3145760 | tf_op jit(solution)/shard_map/ppermute | solution.py:13
  215.1 70.7 %collective-permute-done.3 = bf16[3,2048,256]{2,1,0:T(8,128)(2,1)S(1)} collective-permute-done((bf16[3,2048,256]{2,1,0:T(8,128)(2,1)S(1)}, bf16[3,2048,256]{2,1,0:T(8,128)(2,1)S(1)}, u32[]{:S(2)}, u32[]{:S(2)}) %collective-permute-start.3) | collective-permute-done | bytes 3145760 | tf_op jit(solution)/shard_map/ppermute | solution.py:13
  286.0 9.7 %multiply_add_fusion = f32[3,2048,256]{2,1,0:T(8,128)} fusion(bf16[3,2048,256]{2,1,0:T(8,128)(2,1)S(1)} %convert_element_type.65, bf16[3,2048,256]{2,1,0:T(8,128)(2,1)S(1)} %collective-permute-done.3, bf16[3,2048,256]{2,1,0:T(8,128)(2,1)S(1)} %collective-permute-done.2, bf16[3,2048,256]{2,1,0:T(8,128)(2,1)S(1)} %collective-permute-done.1, ...), kind=kLoop, calls=%fused_computation.18 | loop fusion | flops 58195968 | bytes 37847040 | tf_op jit(solution)/shard_map/add | solution.py:71
  295.7 64.8 %fusion.19 = bf16[1024,3,1,256]{3,0,1,2:T(8,128)(2,1)S(1)} fusion(f32[3,2048,256]{2,1,0:T(8,128)} %multiply_add_fusion), kind=kOutput, calls=%fused_computation.25 | convolution fusion | flops 19358285824 | bytes 7864320 | tf_op jit(solution)/shard_map/kn,sni->ksi/dot_general | solution.py:81
  360.5 53.0 %fusion.22 = bf16[1024,3,1,256]{3,0,1,2:T(8,128)(2,1)S(1)} fusion(f32[3,2048,256]{2,1,0:T(8,128)S(1)} %copy-done), kind=kOutput, calls=%fused_computation.26 | convolution fusion | flops 19359072256 | bytes 7864320 | tf_op jit(solution)/shard_map/kn,sni->ksi/dot_general | solution.py:84
  418.7 98.1 %all-to-all-start = ((bf16[1024,3,2,256]{3,2,1,0:T(2,128)(2,1)}), bf16[1024,3,2,256]{3,2,1,0:T(2,128)(2,1)S(1)}, u32[]{:S(2)}, u32[]{:S(2)}) async-start(bf16[1024,3,2,256]{3,2,1,0:T(2,128)(2,1)} %copy.77), calls=%async_computation | async-start | bytes 6291456 | tf_op jit(solution)/shard_map/all_to_all | solution.py:88
  517.5 71.7 %all-to-all-done = bf16[1024,3,2,256]{3,2,1,0:T(2,128)(2,1)S(1)} async-done(((bf16[1024,3,2,256]{3,2,1,0:T(2,128)(2,1)}), bf16[1024,3,2,256]{3,2,1,0:T(2,128)(2,1)S(1)}, u32[]{:S(2)}, u32[]{:S(2)}) %all-to-all-start) | async-done | bytes 3145760 | tf_op jit(solution)/shard_map/all_to_all | solution.py:88
  601.0 10.9 %all-gather = f32[64,8,192]{2,1,0:T(8,128)} all-gather(f32[16,8,192]{2,1,0:T(8,128)S(1)} %fusion.25), channel_id=2, replica_groups=mesh['freq'=64,'inp'=4] {'inp'}, dimensions={0}, use_global_device_ids=true | all-gather | bytes 491520 | tf_op jit(solution)/shard_map/all_gather | solution.py:20
  614.9 10.6 %psum.28 = f32[16,8,8]{1,2,0:T(8,128)S(1)} all-reduce(f32[16,8,8]{1,2,0:T(8,128)S(1)} %fusion.48), channel_id=1, replica_groups=mesh['freq'=64,'inp'=4] {'inp'}, use_global_device_ids=true, to_apply=%region_1.2 | all-reduce | flops 1024 | bytes 8192 | tf_op jit(solution)/shard_map/psum | solution.py:36
  626.3 12.4 %custom-call.12 = f32[16,8,8]{2,1,0:T(8,128)S(1)} custom-call(f32[16,8,8]{2,1,0:T(8,128)} %fusion.38), custom_call_target="Cholesky" | custom-call | tf_op jit(solution)/shard_map/jit(cholesky)/cholesky | solution.py:37
  638.9 10.0 %custom-call.13 = f32[16,1,8,8]{2,3,1,0:T(8,128)S(1)} custom-call(f32[16,1,8,8]{3,2,1,0:T(8,128)S(1)} %select_bitcast_fusion.3), custom_call_target="InvertDiagBlocksLowerTriangular" | custom-call | tf_op jit(solution)/shard_map/triangular_solve/custom-call.0 | solution.py:38
  652.0 8.5 %all-gather.1 = f32[64,8,192]{2,1,0:T(8,128)} all-gather(f32[16,8,192]{2,1,0:T(8,128)S(1)} %fusion.49), channel_id=3, replica_groups=mesh['freq'=64,'inp'=4] {'inp'}, dimensions={0}, use_global_device_ids=true | all-gather | bytes 491520 | tf_op jit(solution)/shard_map/all_gather | solution.py:20
  663.5 10.6 %psum.29 = f32[16,8,8]{1,2,0:T(8,128)S(1)} all-reduce(f32[16,8,8]{1,2,0:T(8,128)S(1)} %fusion.50), channel_id=1, replica_groups=mesh['freq'=64,'inp'=4] {'inp'}, use_global_device_ids=true, to_apply=%region_5.8 | all-reduce | flops 1024 | bytes 8192 | tf_op jit(solution)/shard_map/psum | solution.py:36
  674.9 12.4 %custom-call.14 = f32[16,8,8]{2,1,0:T(8,128)S(1)} custom-call(f32[16,8,8]{2,1,0:T(8,128)} %fusion.35), custom_call_target="Cholesky" | custom-call | tf_op jit(solution)/shard_map/jit(cholesky)/cholesky | solution.py:37
  687.5 10.0 %custom-call.15 = f32[16,1,8,8]{2,3,1,0:T(8,128)S(1)} custom-call(f32[16,1,8,8]{3,2,1,0:T(8,128)S(1)} %select_bitcast_fusion.2), custom_call_target="InvertDiagBlocksLowerTriangular" | custom-call | tf_op jit(solution)/shard_map/triangular_solve/custom-call.0 | solution.py:38
  700.6 8.1 all-gather.2
  711.7 10.6 %psum.30 = f32[16,8,8]{1,2,0:T(8,128)S(1)} all-reduce(f32[16,8,8]{1,2,0:T(8,128)S(1)} %fusion.52), channel_id=1, replica_groups=mesh['freq'=64,'inp'=4] {'inp'}, use_global_device_ids=true, to_apply=%region_7.10 | all-reduce | flops 1024 | bytes 8192 | tf_op jit(solution)/shard_map/psum | solution.py:36
  723.0 12.4 %custom-call.16 = f32[16,8,8]{2,1,0:T(8,128)S(1)} custom-call(f32[16,8,8]{2,1,0:T(8,128)} %fusion.32), custom_call_target="Cholesky" | custom-call | tf_op jit(solution)/shard_map/jit(cholesky)/cholesky | solution.py:37
  735.7 10.0 %custom-call.17 = f32[16,1,8,8]{2,3,1,0:T(8,128)S(1)} custom-call(f32[16,1,8,8]{3,2,1,0:T(8,128)S(1)} %select_bitcast_fusion.1), custom_call_target="InvertDiagBlocksLowerTriangular" | custom-call | tf_op jit(solution)/shard_map/triangular_solve/custom-call.0 | solution.py:38
  759.8 10.6 %psum.31 = f32[16,8,8]{1,2,0:T(8,128)S(1)} all-reduce(f32[16,8,8]{1,2,0:T(8,128)S(1)} %fusion.54), channel_id=1, replica_groups=mesh['freq'=64,'inp'=4] {'inp'}, use_global_device_ids=true, to_apply=%region_9.12 | all-reduce | flops 1024 | bytes 8192 | tf_op jit(solution)/shard_map/psum | solution.py:36
  771.2 12.4 %custom-call.18 = f32[16,8,8]{2,1,0:T(8,128)S(1)} custom-call(f32[16,8,8]{2,1,0:T(8,128)} %fusion.29), custom_call_target="Cholesky" | custom-call | tf_op jit(solution)/shard_map/jit(cholesky)/cholesky | solution.py:37
  783.8 10.0 %custom-call.19 = f32[16,1,8,8]{2,3,1,0:T(8,128)S(1)} custom-call(f32[16,1,8,8]{3,2,1,0:T(8,128)S(1)} %select_bitcast_fusion), custom_call_target="InvertDiagBlocksLowerTriangular" | custom-call | tf_op jit(solution)/shard_map/triangular_solve/custom-call.0 | solution.py:38
  797.6 8.3 %all-gather.4 = f32[64,8,192]{2,1,0:T(8,128)} all-gather(f32[16,8,192]{2,1,0:T(8,128)S(1)} %fusion.55), channel_id=6, replica_groups=mesh['freq'=64,'inp'=4] {'inp'}, dimensions={0}, use_global_device_ids=true | all-gather | bytes 491520 | tf_op jit(solution)/shard_map/all_gather | solution.py:20
  (77 shorter events, 86.0 us)
Async XLA Ops:
  0.6 15.1 %copy-start.2 = (f32[12,2048]{1,0:T(8,128)S(1)}, f32[12,2048]{1,0:T(8,128)}, u32[]{:S(2)}) copy-start(f32[12,2048]{1,0:T(8,128)} %param.7) | copy-start | bytes 294916
  4.0 193.6 %collective-permute-start.1 = (bf16[3,2048,256]{2,1,0:T(8,128)(2,1)S(1)}, bf16[3,2048,256]{2,1,0:T(8,128)(2,1)S(1)}, u32[]{:S(2)}, u32[]{:S(2)}) collective-permute-start(bf16[3,2048,256]{2,1,0:T(8,128)(2,1)S(1)} %convert_element_type.65), channel_id=1, source_target_pairs={{0,12},{4,16},{8,20},{12,24},{16,28},{20,32},{24,36},{28,40},{32,4... | collective-permute-start | bytes 9437192 | tf_op jit(solution)/shard_map/ppermute | solution.py:13
  9.0 205.7 %collective-permute-start.2 = (bf16[3,2048,256]{2,1,0:T(8,128)(2,1)S(1)}, bf16[3,2048,256]{2,1,0:T(8,128)(2,1)S(1)}, u32[]{:S(2)}, u32[]{:S(2)}) collective-permute-start(bf16[3,2048,256]{2,1,0:T(8,128)(2,1)S(1)} %convert_element_type.65), channel_id=1, source_target_pairs={{0,8},{4,12},{8,16},{12,20},{16,24},{20,28},{24,32},{28,36},{32,40... | collective-permute-start | bytes 9437192 | tf_op jit(solution)/shard_map/ppermute | solution.py:13
  10.6 275.1 %collective-permute-start.3 = (bf16[3,2048,256]{2,1,0:T(8,128)(2,1)S(1)}, bf16[3,2048,256]{2,1,0:T(8,128)(2,1)S(1)}, u32[]{:S(2)}, u32[]{:S(2)}) collective-permute-start(bf16[3,2048,256]{2,1,0:T(8,128)(2,1)S(1)} %convert_element_type.65), channel_id=1, source_target_pairs={{0,4},{4,8},{8,12},{12,16},{16,20},{20,24},{24,28},{28,32},{32,36}... | collective-permute-start | bytes 9437192 | tf_op jit(solution)/shard_map/ppermute | solution.py:13
  12.4 185.1 %collective-permute-start = (bf16[2,2048,256]{2,1,0:T(8,128)(2,1)S(1)}, bf16[2,2048,256]{2,1,0:T(8,128)(2,1)S(1)}, u32[]{:S(2)}, u32[]{:S(2)}) collective-permute-start(bf16[2,2048,256]{2,1,0:T(8,128)(2,1)S(1)} %slice.98), channel_id=1, source_target_pairs={{0,16},{4,20},{8,24},{12,28},{16,32},{20,36},{24,40},{28,44},{32,4... | collective-permute-start | bytes 6291464 | tf_op jit(solution)/shard_map/ppermute | solution.py:13
  295.7 64.8 %copy-start = (f32[3,2048,256]{2,1,0:T(8,128)S(1)}, f32[3,2048,256]{2,1,0:T(8,128)}, u32[]{:S(2)}) copy-start(f32[3,2048,256]{2,1,0:T(8,128)} %multiply_add_fusion) | copy-start | bytes 18874372
  418.7 170.6 %all-to-all-start = ((bf16[1024,3,2,256]{3,2,1,0:T(2,128)(2,1)}), bf16[1024,3,2,256]{3,2,1,0:T(2,128)(2,1)S(1)}, u32[]{:S(2)}, u32[]{:S(2)}) async-start(bf16[1024,3,2,256]{3,2,1,0:T(2,128)(2,1)} %copy.77), calls=%async_computation | async-start | bytes 6291456 | tf_op jit(solution)/shard_map/all_to_all | solution.py:88
  794.4 0.7 copy-start.1
